TPU v7x, 32 devices: a whole 2x2x4 slice. The times are simulated.
32 devices in a mesh: layer: 2 (over core), prow: 4 (over z), pcol: 4 (over y, x).
Axes of the slice: x: 2, y: 2, z: 4, core: 2. Of those that a mesh axis runs over, the one named last changes fastest.
Arguments:
- diag_inverse: float32 [2, 3, 2048, 2048], P('layer', None, 'prow', 'pcol'), may hold values from -1 to 1, as said below
- root_inverse: float32 [2048, 2048], P('prow', 'pcol'), may hold values from -1 to 1, as said below
- coupling: float32 [2, 5, 2048, 2048], P('layer', None, 'prow', 'pcol'), may hold values from -0.0625 to 0.0625
- tile_mask: int32 [2, 5, 16, 16], P('layer'), may hold values 0 or 1
- sketch: float32 [2, 3, 2048, 256], P('layer', None, 'prow'), may hold values from -6 to 6
- root_sketch: float32 [2048, 256], P('prow'), may hold values from -6 to 6
Outputs:
- solution: float32 [2, 3, 2048, 256], P('layer', None, 'prow')
- root_solution: float32 [2048, 256], P('prow')
Inputs may be any that keep to these rules, and one draw needn't show every extreme that they name: `diag_inverse`: lower triangular. `root_inverse`: lower triangular.
All inputs are finite; a program needn't handle non-finite values. No bound on the sum of `tile_mask` on one device may be relied on, other than what follows from the above.
Results may differ from a plain program's by a relative error of at most 0.0001.
Values sent between devices are 32-bit elements; how exact they have to be, the bound alone decides.
No kernel may reach another device: no remote copies, remote signals or barrier semaphores. Data moves between devices by JAX's collectives and lax.ppermute only.
A program may use at most 64 MiB of HBM per device.

v0:
```python
import jax
import jax.numpy as jnp
from jax import lax
from jax.sharding import PartitionSpec as P

TILE = 128


def broadcast(block, axis, owner):
    block = jnp.where(lax.axis_index(axis) == owner, block, jnp.zeros_like(block))
    return lax.psum(block, axis)


def forward_product(matrix, vector):
    return jnp.einsum("nij,njk->nik", matrix, vector, precision=lax.Precision.HIGHEST)


def transpose_product(matrix, vector):
    return jnp.einsum("nij,nik->njk", matrix, vector, precision=lax.Precision.HIGHEST)


def column_panel(vector):
    group_ratio = lax.axis_size("pcol") // lax.axis_size("prow")
    col_index = lax.axis_index("pcol")
    received = broadcast(vector, "prow", col_index // group_ratio)
    col_width = vector.shape[1] // group_ratio
    return lax.dynamic_slice_in_dim(received, col_index % group_ratio * col_width, col_width, 1)


def column_total(partial_value):
    return lax.psum(partial_value, "pcol")


def regroup(column_rows):
    group_ratio = lax.axis_size("pcol") // lax.axis_size("prow")
    row_index = lax.axis_index("prow")
    col_width = column_rows.shape[1]
    complete = lax.all_gather(column_rows, "pcol", axis=1, tiled=True)
    return lax.dynamic_slice_in_dim(
        complete, row_index * (col_width * group_ratio), col_width * group_ratio, 1
    )


def row_total(partial_value):
    return regroup(lax.psum(partial_value, "prow"))


def local_mask(tile_mask, rows_here, cols_here):
    row_tiles = (lax.axis_index("prow") * rows_here + lax.iota(jnp.int32, rows_here)) // TILE
    col_tiles = (lax.axis_index("pcol") * cols_here + lax.iota(jnp.int32, cols_here)) // TILE
    table = jnp.take(tile_mask[0], row_tiles, axis=1)
    table = jnp.take(table, col_tiles, axis=2)
    return table.astype(jnp.float32)


def per_device(diag_inverse, root_inverse, coupling, tile_mask, sketch, root_sketch):
    layer_inverse = diag_inverse[0]
    rows_here = coupling.shape[2]
    cols_here = coupling.shape[3]
    blocks = coupling[0] * local_mask(tile_mask, rows_here, cols_here)
    rhs_local = sketch[0]
    leaves = column_total(forward_product(layer_inverse[0:2], column_panel(rhs_local[0:2])))
    fed_leaves = column_panel(leaves)
    mid_part = forward_product(blocks[0:2], fed_leaves)
    root_part = forward_product(blocks[2:4], fed_leaves)
    mid_rhs = rhs_local[2] - column_total(mid_part[0] + mid_part[1])
    middle = column_total(forward_product(layer_inverse[2:3], column_panel(mid_rhs[None])))[0]
    upper_part = forward_product(blocks[4:5], column_panel(middle[None]))[0]
    update = lax.psum(root_part[0] + root_part[1] + upper_part, ("layer", "pcol"))
    root_forward = column_total(
        forward_product(root_inverse[None], column_panel((root_sketch - update)[None]))
    )[0]
    root_solution = row_total(transpose_product(root_inverse[None], root_forward[None]))[0]
    spread_root = jnp.broadcast_to(root_solution, (3,) + root_solution.shape)
    back_terms = row_total(transpose_product(blocks[2:5], spread_root))
    mid_back = middle - back_terms[2]
    mid_solution = row_total(transpose_product(layer_inverse[2:3], mid_back[None]))[0]
    spread_mid = jnp.broadcast_to(mid_solution, (2,) + mid_solution.shape)
    leaf_terms = row_total(transpose_product(blocks[0:2], spread_mid))
    leaf_back = leaves - leaf_terms - back_terms[0:2]
    leaf_solution = row_total(transpose_product(layer_inverse[0:2], leaf_back))
    solution = jnp.concatenate([leaf_solution, mid_solution[None]], axis=0)[None]
    return (solution, root_solution)


def solution(mesh):
    in_specs = (
        P("layer", None, "prow", "pcol"),
        P("prow", "pcol"),
        P("layer", None, "prow", "pcol"),
        P("layer", None, None, None),
        P("layer", None, "prow", None),
        P("prow", None),
    )
    out_specs = (P("layer", None, "prow", None), P("prow", None))
    return jax.shard_map(
        per_device, mesh=mesh, in_specs=in_specs, out_specs=out_specs, check_vma=False
    )
```

profile of v0, /device:TPU:0, one launch (start us, length us, event | category | flops | bytes accessed | tf_op | source)
XLA Modules:
  0.0 1045.1 jit_solution(8067346142498596732)
XLA Ops:
  7.2 1.4 slice.51
  9.0 1.1 select_bitcast_fusion.1
  10.1 55.4 %all-reduce.16.cloned.1.call-done = f32[2,512,256]{1,2,0:T(8,128)} async-done(((f32[2,512,256]{1,2,0:T(8,128)}), f32[2,512,256]{1,2,0:T(8,128)}) %all-reduce.16.cloned.1.call-update) | async-done | bytes 1048592 | tf_op jit(solution)/shard_map/psum | solution.py:11
  65.5 4.8 fusion.6
  70.5 2.7 gather_fusion
  73.2 49.2 %all-reduce.18.cloned.1.call-done = f32[2,512,256]{1,2,0:T(8,128)} async-done(((f32[2,512,256]{1,2,0:T(8,128)}), f32[2,512,256]{1,2,0:T(8,128)}) %all-reduce.18.cloned.1.call-update) | async-done | bytes 1048592 | tf_op jit(solution)/shard_map/psum | solution.py:31
  122.5 2.3 broadcast_select_fusion
  124.8 3.4 select_bitcast_fusion
  128.2 0.8 copy.16
  129.0 4.4 gather_fusion.1
  133.4 8.8 copy.17
  142.2 7.9 bitcast_multiply_fusion
  150.1 27.3 %all-reduce.20.cloned.1.call-done = f32[2,512,256]{1,2,0:T(8,128)} async-done(((f32[2,512,256]{1,2,0:T(8,128)}), f32[2,512,256]{1,2,0:T(8,128)}) %all-reduce.20.cloned.1.call-update) | async-done | bytes 1048592 | tf_op jit(solution)/shard_map/psum | solution.py:11
  177.4 3.8 fusion.35
  181.2 0.9 fusion.23
  182.2 44.8 %all-reduce.22.cloned.1.call-done = f32[512,256]{1,0:T(8,128)} async-done(((f32[512,256]{1,0:T(8,128)}), f32[512,256]{1,0:T(8,128)}) %all-reduce.22.cloned.1.call-update) | async-done | bytes 524304 | tf_op jit(solution)/shard_map/psum | solution.py:31
  227.0 2.1 fusion.24
  229.1 39.0 %all-reduce.24.cloned.1.call-done = f32[512,256]{1,0:T(8,128)} async-done(((f32[512,256]{1,0:T(8,128)}), f32[512,256]{1,0:T(8,128)}) %all-reduce.24.cloned.1.call-update) | async-done | bytes 524304 | tf_op jit(solution)/shard_map/psum | solution.py:11
  268.1 4.0 convolution_bitcast_fusion.3
  272.2 45.4 %all-reduce.26.cloned.1.call-done = f32[1,512,256]{1,2,0:T(8,128)} async-done(((f32[1,512,256]{1,2,0:T(8,128)}), f32[1,512,256]{1,2,0:T(8,128)}) %all-reduce.26.cloned.1.call-update) | async-done | bytes 524304 | tf_op jit(solution)/shard_map/psum | solution.py:31
  317.6 1.9 select_bitcast_fusion.2
  319.8 3.6 fusion.36
  323.4 35.5 %all-reduce.28.cloned.1.call-done = f32[512,256]{0,1:T(8,128)} async-done(((f32[512,256]{0,1:T(8,128)}), f32[512,256]{0,1:T(8,128)}) %all-reduce.28.cloned.1.call-update) | async-done | bytes 524304 | tf_op jit(solution)/shard_map/psum | solution.py:11
  358.9 3.2 convolution_add_fusion
  362.1 55.0 %all-reduce.30.cloned.1.call-done = f32[512,256]{1,0:T(8,128)} async-done(((f32[512,256]{1,0:T(8,128)}), f32[512,256]{1,0:T(8,128)}) %all-reduce.30.cloned.1.call-update) | async-done | bytes 524304 | tf_op jit(solution)/shard_map/psum | solution.py:69
  417.1 1.9 subtract_select_fusion
  419.1 38.7 %all-reduce.32.cloned.1.call-done = f32[512,256]{1,0:T(8,128)} async-done(((f32[512,256]{1,0:T(8,128)}), f32[512,256]{1,0:T(8,128)}) %all-reduce.32.cloned.1.call-update) | async-done | bytes 524304 | tf_op jit(solution)/shard_map/psum | solution.py:11
  457.8 3.7 convolution_bitcast_fusion.2
  461.6 45.4 %all-reduce.34.cloned.1.call-done = f32[512,256]{0,1:T(8,128)} async-done(((f32[512,256]{0,1:T(8,128)}), f32[512,256]{0,1:T(8,128)}) %all-reduce.34.cloned.1.call-update) | async-done | bytes 524304 | tf_op jit(solution)/shard_map/psum | solution.py:31
  507.0 2.9 convolution_bitcast_fusion.1
  510.0 38.4 %all-reduce.36.cloned.1.call-done = f32[1,512,256]{1,2,0:T(8,128)} async-done(((f32[1,512,256]{1,2,0:T(8,128)}), f32[1,512,256]{1,2,0:T(8,128)}) %all-reduce.36.cloned.1.call-update) | async-done | bytes 524304 | tf_op jit(solution)/shard_map/psum | solution.py:45
  548.5 37.1 %all-gather.6.cloned.1.call-done = f32[1,2048,256]{1,2,0:T(8,128)} async-done(((f32[1,512,256]{1,2,0:T(8,128)}), f32[1,2048,256]{1,2,0:T(8,128)}) %all-gather.6.cloned.1.call-update) | async-done | bytes 2097168 | tf_op jit(solution)/shard_map/all_gather | solution.py:38
  585.6 1.1 constant_dynamic-slice_fusion.2
  586.9 6.1 fusion.18
  593.1 69.2 %all-reduce.38.cloned.1.call-done = f32[3,512,256]{1,2,0:T(8,128)} async-done(((f32[3,512,256]{1,2,0:T(8,128)}), f32[3,512,256]{1,2,0:T(8,128)}) %all-reduce.38.cloned.1.call-update) | async-done | bytes 1572880 | tf_op jit(solution)/shard_map/psum | solution.py:45
  662.4 71.0 %all-gather.8.cloned.1.call-done = f32[3,2048,256]{1,2,0:T(8,128)} async-done(((f32[3,512,256]{1,2,0:T(8,128)}), f32[3,2048,256]{1,2,0:T(8,128)}) %all-gather.8.cloned.1.call-update) | async-done | bytes 6291472 | tf_op jit(solution)/shard_map/all_gather | solution.py:38
  733.4 3.3 convolution_bitcast_fusion
  736.7 38.4 %all-reduce.40.cloned.1.call-done = f32[1,512,256]{1,2,0:T(8,128)} async-done(((f32[1,512,256]{1,2,0:T(8,128)}), f32[1,512,256]{1,2,0:T(8,128)}) %all-reduce.40.cloned.1.call-update) | async-done | bytes 524304 | tf_op jit(solution)/shard_map/psum | solution.py:45
  775.4 36.9 %all-gather.10.cloned.1.call-done = f32[1,2048,256]{1,2,0:T(8,128)} async-done(((f32[1,512,256]{1,2,0:T(8,128)}), f32[1,2048,256]{1,2,0:T(8,128)}) %all-gather.10.cloned.1.call-update) | async-done | bytes 2097168 | tf_op jit(solution)/shard_map/all_gather | solution.py:38
  812.3 1.1 constant_dynamic-slice_fusion.1
  813.6 4.7 fusion.25
  818.3 51.9 %all-reduce.42.cloned.1.call-done = f32[2,512,256]{1,2,0:T(8,128)} async-done(((f32[2,512,256]{1,2,0:T(8,128)}), f32[2,512,256]{1,2,0:T(8,128)}) %all-reduce.42.cloned.1.call-update) | async-done | bytes 1048592 | tf_op jit(solution)/shard_map/psum | solution.py:45
  870.3 53.8 %all-gather.12.cloned.1.call-done = f32[2,2048,256]{1,2,0:T(8,128)} async-done(((f32[2,512,256]{1,2,0:T(8,128)}), f32[2,2048,256]{1,2,0:T(8,128)}) %all-gather.12.cloned.1.call-update) | async-done | bytes 4194320 | tf_op jit(solution)/shard_map/all_gather | solution.py:38
  924.1 5.2 fusion.9
  929.3 51.9 %all-reduce.44.cloned.1.call-done = f32[2,512,256]{1,2,0:T(8,128)} async-done(((f32[2,512,256]{1,2,0:T(8,128)}), f32[2,512,256]{1,2,0:T(8,128)}) %all-reduce.44.cloned.1.call-update) | async-done | bytes 1048592 | tf_op jit(solution)/shard_map/psum | solution.py:45
  981.3 53.9 %all-gather.14.cloned.1.call-done = f32[2,2048,256]{1,2,0:T(8,128)} async-done(((f32[2,512,256]{1,2,0:T(8,128)}), f32[2,2048,256]{1,2,0:T(8,128)}) %all-gather.14.cloned.1.call-update) | async-done | bytes 4194320 | tf_op jit(solution)/shard_map/all_gather | solution.py:38
  1035.2 1.3 constant_dynamic-slice_fusion
  1036.7 1.6 copy.24
  (64 shorter events, 2.5 us)
Async XLA Ops:
  7.2 450.6 %copy-start = (f32[512,512]{1,0:T(8,128)S(1)}, f32[512,512]{1,0:T(8,128)}, u32[]{:S(2)}) copy-start(f32[512,512]{1,0:T(8,128)} %param.7) | copy-start | bytes 3145732
  7.2 58.3 %all-reduce.16.cloned.1.call-start = ((), (), s32[]{:S(2)}) async-start(), calls=%async_computation | async-start | bytes 2097152 | tf_op jit(solution)/shard_map/psum | solution.py:11
  10.0 60.4 %copy-start.6 = (s32[1,5,16,16]{3,2,1,0:T(8,128)S(1)}, s32[1,5,16,16]{3,2,1,0:T(8,128)}, u32[]{:S(2)}) copy-start(s32[1,5,16,16]{3,2,1,0:T(8,128)} %param.9) | copy-start | bytes 15364
  10.0 112.4 %all-reduce.18.cloned.1.call-start = ((), (), s32[]{:S(2)}) async-start(), calls=%async_computation.1 | async-start | bytes 2097152 | tf_op jit(solution)/shard_map/psum | solution.py:31
  70.4 107.0 %all-reduce.20.cloned.1.call-start = ((), (), s32[]{:S(2)}) async-start(), calls=%async_computation.2 | async-start | bytes 2097152 | tf_op jit(solution)/shard_map/psum | solution.py:11
  124.8 102.2 %all-reduce.22.cloned.1.call-start = ((), (), s32[]{:S(2)}) async-start(), calls=%async_computation.3 | async-start | bytes 1048576 | tf_op jit(solution)/shard_map/psum | solution.py:31
  182.1 137.7 %copy-start.2 = (f32[2,512,256]{1,2,0:T(8,128)S(1)}, f32[2,512,256]{1,2,0:T(8,128)}, u32[]{:S(2)}) copy-start(f32[2,512,256]{1,2,0:T(8,128)} %all-reduce.20.cloned.1.call-done) | copy-start | bytes 3145732
  182.1 86.0 %all-reduce.24.cloned.1.call-start = ((), (), s32[]{:S(2)}) async-start(), calls=%async_computation.4 | async-start | bytes 1048576 | tf_op jit(solution)/shard_map/psum | solution.py:11
  229.0 88.6 %all-reduce.26.cloned.1.call-start = ((), (), s32[]{:S(2)}) async-start(), calls=%async_computation.5 | async-start | bytes 1048576 | tf_op jit(solution)/shard_map/psum | solution.py:31
  272.1 86.7 %all-reduce.28.cloned.1.call-start = ((), (), s32[]{:S(2)}) async-start(), calls=%async_computation.6 | async-start | bytes 1048576 | tf_op jit(solution)/shard_map/psum | solution.py:11
  319.5 97.6 %all-reduce.30.cloned.1.call-start = ((), (), s32[]{:S(2)}) async-start(), calls=%async_computation.7 | async-start | bytes 1048576 | tf_op jit(solution)/shard_map/psum | solution.py:69
  323.3 93.8 %copy-start.5 = (f32[512,256]{1,0:T(8,128)S(1)}, f32[512,256]{1,0:T(8,128)}, u32[]{:S(2)}) copy-start(f32[512,256]{1,0:T(8,128)} %param.11) | copy-start | bytes 1572868
  362.1 95.7 %all-reduce.32.cloned.1.call-start = ((), (), s32[]{:S(2)}) async-start(), calls=%async_computation.8 | async-start | bytes 1048576 | tf_op jit(solution)/shard_map/psum | solution.py:11
  419.1 88.0 %all-reduce.34.cloned.1.call-start = ((), (), s32[]{:S(2)}) async-start(), calls=%async_computation.9 | async-start | bytes 1048576 | tf_op jit(solution)/shard_map/psum | solution.py:31
  461.5 86.9 %all-reduce.36.cloned.1.call-start = ((), (), s32[]{:S(2)}) async-start(), calls=%async_computation.10 | async-start | bytes 1048576 | tf_op jit(solution)/shard_map/psum | solution.py:45
  509.9 75.6 %all-gather.6.cloned.1.call-start = ((), (), s32[]{:S(2)}) async-start(), calls=%async_computation.11 | async-start | bytes 2621440 | tf_op jit(solution)/shard_map/all_gather | solution.py:38
  548.4 113.9 %all-reduce.38.cloned.1.call-start = ((), (), s32[]{:S(2)}) async-start(), calls=%async_computation.12 | async-start | bytes 3145728 | tf_op jit(solution)/shard_map/psum | solution.py:45
  586.9 6.2 copy-start.3
  593.0 140.4 %copy-start.4 = (f32[1,512,256]{1,2,0:T(8,128)S(1)}, f32[1,512,256]{1,2,0:T(8,128)}, u32[]{:S(2)}) copy-start(f32[1,512,256]{1,2,0:T(8,128)} %all-reduce.26.cloned.1.call-done) | copy-start | bytes 1572868
  593.0 140.3 %all-gather.8.cloned.1.call-start = ((), (), s32[]{:S(2)}) async-start(), calls=%async_computation.13 | async-start | bytes 7864320 | tf_op jit(solution)/shard_map/all_gather | solution.py:38
  662.3 112.8 %all-reduce.40.cloned.1.call-start = ((), (), s32[]{:S(2)}) async-start(), calls=%async_computation.14 | async-start | bytes 1048576 | tf_op jit(solution)/shard_map/psum | solution.py:45
  736.7 75.6 %all-gather.10.cloned.1.call-start = ((), (), s32[]{:S(2)}) async-start(), calls=%async_computation.15 | async-start | bytes 2621440 | tf_op jit(solution)/shard_map/all_gather | solution.py:38
  775.1 95.1 %all-reduce.42.cloned.1.call-start = ((), (), s32[]{:S(2)}) async-start(), calls=%async_computation.16 | async-start | bytes 2097152 | tf_op jit(solution)/shard_map/psum | solution.py:45
  813.6 110.5 %copy-start.1 = (f32[2,512,256]{1,2,0:T(8,128)S(1)}, f32[2,512,256]{1,2,0:T(8,128)}, u32[]{:S(2)}) copy-start(f32[2,512,256]{1,2,0:T(8,128)} %all-reduce.18.cloned.1.call-done) | copy-start | bytes 3145732
  818.3 105.8 %all-gather.12.cloned.1.call-start = ((), (), s32[]{:S(2)}) async-start(), calls=%async_computation.17 | async-start | bytes 5242880 | tf_op jit(solution)/shard_map/all_gather | solution.py:38
  870.3 111.0 %all-reduce.44.cloned.1.call-start = ((), (), s32[]{:S(2)}) async-start(), calls=%async_computation.18 | async-start | bytes 2097152 | tf_op jit(solution)/shard_map/psum | solution.py:45
  929.3 105.9 %all-gather.14.cloned.1.call-start = ((), (), s32[]{:S(2)}) async-start(), calls=%async_computation.19 | async-start | bytes 5242880 | tf_op jit(solution)/shard_map/all_gather | solution.py:38
Sparse Core Ops, SparseCore 0:
  11.0 54.5 all-reduce.15
  70.5 51.9 all-reduce.17
  125.5 51.8 all-reduce.19
  182.2 44.6 all-reduce.21
  229.7 38.2 all-reduce.23
  272.3 45.3 all-reduce.25
  320.5 38.2 all-reduce.27
  362.5 54.5 all-reduce.29
  420.2 37.5 all-reduce.31
  461.6 45.3 all-reduce.33
  510.1 38.2 all-reduce.35
  550.2 35.2 all-gather.5
  593.2 69.0 all-reduce.37
  664.1 69.1 all-gather.7
  736.8 38.2 all-reduce.39
  777.0 35.2 all-gather.9
  818.4 51.8 all-reduce.41
  872.0 52.0 all-gather.11
  929.4 51.8 all-reduce.43
  983.1 52.0 all-gather.13
where the time goes:
time: 1050 us
  waiting for transfers between devices  939 us (89%)
  matrix products  45.3 us (4%)
  local copies, waits for them, and re-layouts  23.8 us (2%)
  other arithmetic  21.5 us (2%)
  between operations  14.5 us (1%)
    all_gather x5, waiting for transfers between devices, regroup(): complete = lax.all_gather(column_rows, 'pcol', axis=1, tiled=True)  253 us
    psum x5, waiting for transfers between devices, row_total(): return regroup(lax.psum(partial_value, 'prow'))  250 us
    psum x5, waiting for transfers between devices, broadcast(): return lax.psum(block, axis)  196 us
    psum x4, waiting for transfers between devices, column_total(): return lax.psum(partial_value, 'pcol')  185 us
    psum x1, waiting for transfers between devices, per_device(): lax.psum(root_part[0] + root_part[1] + upper_part, ('layer', 'pcol'))  55 us
    dot_general x6, matrix products, forward_product(): jnp.einsum('nij,njk->nik', matrix, vector, precision=lax.Precision.HIGHEST)  23.2 us
    dot_general x5, matrix products, transpose_product(): jnp.einsum('nij,nik->njk', matrix, vector, precision=lax.Precision.HIGHEST)  22.1 us
  transfers between devices with their start and end apart: 20, of which 20 were waited for; matrix products, arithmetic and copies ran while one was open for 3% of the time, Pallas kernels for 0%

commit v1 on v0

--- a/solution.py
+++ b/solution.py
@@ -35,7 +35,24 @@
     group_ratio = lax.axis_size("pcol") // lax.axis_size("prow")
     row_index = lax.axis_index("prow")
     col_width = column_rows.shape[1]
-    complete = lax.all_gather(column_rows, "pcol", axis=1, tiled=True)
+    size, index, rows = (lax.axis_size("pcol"), lax.axis_index("pcol"), column_rows.shape[1])
+    upward = [(i, (i + 1) % size) for i in range(size)]
+    behind = [(i, (i - 1) % size) for i in range(size)]
+    out = jnp.zeros(
+        (*column_rows.shape[:1], size * rows, *column_rows.shape[1 + 1 :]), column_rows.dtype
+    )
+    out = lax.dynamic_update_slice_in_dim(out, column_rows, index * rows, axis=1)
+    from_left = from_right = column_rows
+    middle_2 = size // 2
+    for step in range(1, middle_2 + 1):
+        from_left = lax.ppermute(from_left, "pcol", upward)
+        out = lax.dynamic_update_slice_in_dim(out, from_left, (index - step) % size * rows, axis=1)
+        if step < size - middle_2:
+            from_right = lax.ppermute(from_right, "pcol", behind)
+            out = lax.dynamic_update_slice_in_dim(
+                out, from_right, (index + step) % size * rows, axis=1
+            )
+    complete = out
     return lax.dynamic_slice_in_dim(
         complete, row_index * (col_width * group_ratio), col_width * group_ratio, 1
     )

time: 1050 us -> 1110 us (1.057)
  waiting for transfers between devices: 939 us -> 974 us
  starting transfers between devices: 1.22 us -> 18.3 us
    ppermute x0 -> x15, waiting for transfers between devices: none -> 292 us  [the longest x10 201 us: regroup(): from_left = lax.ppermute(from_left, 'pcol', upward)]
    all_gather x5 -> x0, waiting for transfers between devices: 253 us -> none  [regroup(): complete = lax.all_gather(column_rows, 'pcol', axis=1, tiled=True)]
    ppermute x0 -> x15, starting transfers between devices: none -> 17.5 us  [the longest x10 10.2 us: regroup(): from_left = lax.ppermute(from_left, 'pcol', upward)]
  transfers between devices with their start and end apart: 20 -> 30, of which waited for: 20 -> 30; matrix products, arithmetic and copies ran while one was open for 3% -> 4% of each run, Pallas kernels for 0% -> 0%
where the time goes in v1:
time: 1110 us
  waiting for transfers between devices  974 us (88%)
  matrix products  44.1 us (4%)
  local copies, waits for them, and re-layouts  33.4 us (3%)
  other arithmetic  21.7 us (2%)
  starting transfers between devices  18.3 us (2%)
  between operations  14.4 us (1%)
    psum x5, waiting for transfers between devices, row_total(): return regroup(lax.psum(partial_value, 'prow'))  245 us
    ppermute x10, waiting for transfers between devices, regroup(): from_left = lax.ppermute(from_left, 'pcol', upward)  201 us
    psum x5, waiting for transfers between devices, broadcast(): return lax.psum(block, axis)  196 us
    psum x4, waiting for transfers between devices, column_total(): return lax.psum(partial_value, 'pcol')  185 us
    ppermute x5, waiting for transfers between devices, regroup(): from_right = lax.ppermute(from_right, 'pcol', behind)  91.6 us
    psum x1, waiting for transfers between devices, per_device(): lax.psum(root_part[0] + root_part[1] + upper_part, ('layer', 'pcol'))  55 us
    dot_general x6, matrix products, forward_product(): jnp.einsum('nij,njk->nik', matrix, vector, precision=lax.Precision.HIGHEST)  23.2 us
  transfers between devices with their start and end apart: 30, of which 30 were waited for; matrix products, arithmetic and copies ran while one was open for 4% of the time, Pallas kernels for 0%

profile of v1, /device:TPU:0, one launch (start us, length us, event | category | flops | bytes accessed | tf_op | source)
XLA Modules:
  0.0 1105.4 jit_solution(3638670156169952454)
XLA Ops:
  10.1 55.4 %all-reduce.16.cloned.1.call-done = f32[2,512,256]{1,2,0:T(8,128)} async-done(((f32[2,512,256]{1,2,0:T(8,128)}), f32[2,512,256]{1,2,0:T(8,128)}) %all-reduce.16.cloned.1.call-update) | async-done | bytes 1048592 | tf_op jit(solution)/shard_map/psum | solution.py:11
  65.5 4.8 fusion.6
  70.5 2.7 gather_fusion
  73.2 49.2 %all-reduce.18.cloned.1.call-done = f32[2,512,256]{1,2,0:T(8,128)} async-done(((f32[2,512,256]{1,2,0:T(8,128)}), f32[2,512,256]{1,2,0:T(8,128)}) %all-reduce.18.cloned.1.call-update) | async-done | bytes 1048592 | tf_op jit(solution)/shard_map/psum | solution.py:31
  122.5 2.3 broadcast_select_fusion
  124.8 3.4 select_bitcast_fusion
  129.0 4.5 gather_fusion.1
  133.4 8.7 copy.19
  142.2 7.9 bitcast_multiply_fusion
  150.1 27.3 %all-reduce.20.cloned.1.call-done = f32[2,512,256]{1,2,0:T(8,128)} async-done(((f32[2,512,256]{1,2,0:T(8,128)}), f32[2,512,256]{1,2,0:T(8,128)}) %all-reduce.20.cloned.1.call-update) | async-done | bytes 1048592 | tf_op jit(solution)/shard_map/psum | solution.py:11
  177.4 3.8 fusion.35
  182.2 44.8 %all-reduce.22.cloned.1.call-done = f32[512,256]{1,0:T(8,128)} async-done(((f32[512,256]{1,0:T(8,128)}), f32[512,256]{1,0:T(8,128)}) %all-reduce.22.cloned.1.call-update) | async-done | bytes 524304 | tf_op jit(solution)/shard_map/psum | solution.py:31
  229.1 39.0 %all-reduce.24.cloned.1.call-done = f32[512,256]{1,0:T(8,128)} async-done(((f32[512,256]{1,0:T(8,128)}), f32[512,256]{1,0:T(8,128)}) %all-reduce.24.cloned.1.call-update) | async-done | bytes 524304 | tf_op jit(solution)/shard_map/psum | solution.py:11
  268.1 4.0 convolution_bitcast_fusion.3
  272.2 45.4 %all-reduce.26.cloned.1.call-done = f32[1,512,256]{1,2,0:T(8,128)} async-done(((f32[1,512,256]{1,2,0:T(8,128)}), f32[1,512,256]{1,2,0:T(8,128)}) %all-reduce.26.cloned.1.call-update) | async-done | bytes 524304 | tf_op jit(solution)/shard_map/psum | solution.py:31
  319.8 3.6 fusion.36
  323.4 35.5 %all-reduce.28.cloned.1.call-done = f32[512,256]{0,1:T(8,128)} async-done(((f32[512,256]{0,1:T(8,128)}), f32[512,256]{0,1:T(8,128)}) %all-reduce.28.cloned.1.call-update) | async-done | bytes 524304 | tf_op jit(solution)/shard_map/psum | solution.py:11
  358.9 3.2 convolution_add_fusion
  362.1 55.0 %all-reduce.30.cloned.1.call-done = f32[512,256]{1,0:T(8,128)} async-done(((f32[512,256]{1,0:T(8,128)}), f32[512,256]{1,0:T(8,128)}) %all-reduce.30.cloned.1.call-update) | async-done | bytes 524304 | tf_op jit(solution)/shard_map/psum | solution.py:86
  419.3 38.5 %all-reduce.32.cloned.1.call-done = f32[512,256]{1,0:T(8,128)} async-done(((f32[512,256]{1,0:T(8,128)}), f32[512,256]{1,0:T(8,128)}) %all-reduce.32.cloned.1.call-update) | async-done | bytes 524304 | tf_op jit(solution)/shard_map/psum | solution.py:11
  457.8 3.7 convolution_bitcast_fusion.2
  461.6 45.4 %all-reduce.34.cloned.1.call-done = f32[512,256]{0,1:T(8,128)} async-done(((f32[512,256]{0,1:T(8,128)}), f32[512,256]{0,1:T(8,128)}) %all-reduce.34.cloned.1.call-update) | async-done | bytes 524304 | tf_op jit(solution)/shard_map/psum | solution.py:31
  507.0 2.9 convolution_bitcast_fusion.1
  510.0 38.4 %all-reduce.36.cloned.1.call-done = f32[1,512,256]{1,2,0:T(8,128)} async-done(((f32[1,512,256]{1,2,0:T(8,128)}), f32[1,512,256]{1,2,0:T(8,128)}) %all-reduce.36.cloned.1.call-update) | async-done | bytes 524304 | tf_op jit(solution)/shard_map/psum | solution.py:62
  551.3 13.0 %collective-permute-done = f32[1,512,256]{1,2,0:T(8,128)S(1)} collective-permute-done((f32[1,512,256]{1,2,0:T(8,128)}, f32[1,512,256]{1,2,0:T(8,128)S(1)}, u32[]{:S(2)}, u32[]{:S(2)}) %collective-permute-start) | collective-permute-done | bytes 524320 | tf_op jit(solution)/shard_map/ppermute | solution.py:48
  566.3 9.3 collective-permute-done.1
  575.7 9.0 collective-permute-done.2
  585.0 6.1 fusion.18
  591.2 67.9 %all-reduce.38.cloned.1.call-done = f32[3,512,256]{1,2,0:T(8,128)} async-done(((f32[3,512,256]{1,2,0:T(8,128)}), f32[3,512,256]{1,2,0:T(8,128)}) %all-reduce.38.cloned.1.call-update) | async-done | bytes 1572880 | tf_op jit(solution)/shard_map/psum | solution.py:62
  662.1 35.6 %collective-permute-done.3 = f32[3,512,256]{1,2,0:T(8,128)} collective-permute-done((f32[3,512,256]{1,2,0:T(8,128)}, f32[3,512,256]{1,2,0:T(8,128)}, u32[]{:S(2)}, u32[]{:S(2)}) %collective-permute-start.3) | collective-permute-done | bytes 1572896 | tf_op jit(solution)/shard_map/ppermute | solution.py:48
  700.8 30.6 %collective-permute-done.4 = f32[3,512,256]{1,2,0:T(8,128)} collective-permute-done((f32[3,512,256]{1,2,0:T(8,128)}, f32[3,512,256]{1,2,0:T(8,128)}, u32[]{:S(2)}, u32[]{:S(2)}) %collective-permute-start.4) | collective-permute-done | bytes 1572896 | tf_op jit(solution)/shard_map/ppermute | solution.py:51
  732.9 29.8 %collective-permute-done.5 = f32[3,512,256]{1,2,0:T(8,128)} collective-permute-done((f32[3,512,256]{1,2,0:T(8,128)}, f32[3,512,256]{1,2,0:T(8,128)}, u32[]{:S(2)}, u32[]{:S(2)}) %collective-permute-start.5) | collective-permute-done | bytes 1572896 | tf_op jit(solution)/shard_map/ppermute | solution.py:48
  764.3 2.6 copy-done.3
  767.0 3.1 convolution_bitcast_fusion
  770.1 37.8 %all-reduce.40.cloned.1.call-done = f32[1,512,256]{1,2,0:T(8,128)} async-done(((f32[1,512,256]{1,2,0:T(8,128)}), f32[1,512,256]{1,2,0:T(8,128)}) %all-reduce.40.cloned.1.call-update) | async-done | bytes 524304 | tf_op jit(solution)/shard_map/psum | solution.py:62
  810.9 13.0 %collective-permute-done.6 = f32[1,512,256]{1,2,0:T(8,128)S(1)} collective-permute-done((f32[1,512,256]{1,2,0:T(8,128)}, f32[1,512,256]{1,2,0:T(8,128)S(1)}, u32[]{:S(2)}, u32[]{:S(2)}) %collective-permute-start.6) | collective-permute-done | bytes 524320 | tf_op jit(solution)/shard_map/ppermute | solution.py:48
  825.9 9.3 collective-permute-done.7
  835.2 9.0 collective-permute-done.8
  844.6 4.6 fusion.25
  849.2 50.6 %all-reduce.42.cloned.1.call-done = f32[2,512,256]{1,2,0:T(8,128)} async-done(((f32[2,512,256]{1,2,0:T(8,128)}), f32[2,512,256]{1,2,0:T(8,128)}) %all-reduce.42.cloned.1.call-update) | async-done | bytes 1048592 | tf_op jit(solution)/shard_map/psum | solution.py:62
  902.8 24.2 %collective-permute-done.9 = f32[2,512,256]{1,2,0:T(8,128)S(1)} collective-permute-done((f32[2,512,256]{1,2,0:T(8,128)}, f32[2,512,256]{1,2,0:T(8,128)S(1)}, u32[]{:S(2)}, u32[]{:S(2)}) %collective-permute-start.9) | collective-permute-done | bytes 1048608 | tf_op jit(solution)/shard_map/ppermute | solution.py:48
  928.3 21.2 %collective-permute-done.10 = f32[2,512,256]{1,2,0:T(8,128)S(1)} collective-permute-done((f32[2,512,256]{1,2,0:T(8,128)}, f32[2,512,256]{1,2,0:T(8,128)S(1)}, u32[]{:S(2)}, u32[]{:S(2)}) %collective-permute-start.10) | collective-permute-done | bytes 1048608 | tf_op jit(solution)/shard_map/ppermute | solution.py:51
  949.6 21.5 %collective-permute-done.11 = f32[2,512,256]{1,2,0:T(8,128)S(1)} collective-permute-done((f32[2,512,256]{1,2,0:T(8,128)S(1)}, f32[2,512,256]{1,2,0:T(8,128)S(1)}, u32[]{:S(2)}, u32[]{:S(2)}) %collective-permute-start.11) | collective-permute-done | bytes 1048608 | tf_op jit(solution)/shard_map/ppermute | solution.py:48
  971.1 4.2 fusion.9
  975.4 50.4 %all-reduce.44.cloned.1.call-done = f32[2,512,256]{1,2,0:T(8,128)} async-done(((f32[2,512,256]{1,2,0:T(8,128)}), f32[2,512,256]{1,2,0:T(8,128)}) %all-reduce.44.cloned.1.call-update) | async-done | bytes 1048592 | tf_op jit(solution)/shard_map/psum | solution.py:62
  1028.7 24.2 %collective-permute-done.12 = f32[2,512,256]{1,2,0:T(8,128)S(1)} collective-permute-done((f32[2,512,256]{1,2,0:T(8,128)}, f32[2,512,256]{1,2,0:T(8,128)S(1)}, u32[]{:S(2)}, u32[]{:S(2)}) %collective-permute-start.12) | collective-permute-done | bytes 1048608 | tf_op jit(solution)/shard_map/ppermute | solution.py:48
  1054.2 21.2 %collective-permute-done.13 = f32[2,512,256]{1,2,0:T(8,128)S(1)} collective-permute-done((f32[2,512,256]{1,2,0:T(8,128)}, f32[2,512,256]{1,2,0:T(8,128)S(1)}, u32[]{:S(2)}, u32[]{:S(2)}) %collective-permute-start.13) | collective-permute-done | bytes 1048608 | tf_op jit(solution)/shard_map/ppermute | solution.py:51
  1075.5 21.4 %collective-permute-done.14 = f32[2,512,256]{1,2,0:T(8,128)S(1)} collective-permute-done((f32[2,512,256]{1,2,0:T(8,128)S(1)}, f32[2,512,256]{1,2,0:T(8,128)S(1)}, u32[]{:S(2)}, u32[]{:S(2)}) %collective-permute-start.14) | collective-permute-done | bytes 1048608 | tf_op jit(solution)/shard_map/ppermute | solution.py:48
  (114 shorter events, 41.6 us)
Async XLA Ops:
  7.2 450.6 %copy-start = (f32[512,512]{1,0:T(8,128)S(1)}, f32[512,512]{1,0:T(8,128)}, u32[]{:S(2)}) copy-start(f32[512,512]{1,0:T(8,128)} %param.7) | copy-start | bytes 3145732
  7.2 58.3 %all-reduce.16.cloned.1.call-start = ((), (), s32[]{:S(2)}) async-start(), calls=%async_computation | async-start | bytes 2097152 | tf_op jit(solution)/shard_map/psum | solution.py:11
  9.0 61.5 %copy-start.11 = (s32[1,5,16,16]{3,2,1,0:T(8,128)S(1)}, s32[1,5,16,16]{3,2,1,0:T(8,128)}, u32[]{:S(2)}) copy-start(s32[1,5,16,16]{3,2,1,0:T(8,128)} %param.9) | copy-start | bytes 15364
  10.1 112.4 %all-reduce.18.cloned.1.call-start = ((), (), s32[]{:S(2)}) async-start(), calls=%async_computation.1 | async-start | bytes 2097152 | tf_op jit(solution)/shard_map/psum | solution.py:31
  70.4 107.0 %all-reduce.20.cloned.1.call-start = ((), (), s32[]{:S(2)}) async-start(), calls=%async_computation.2 | async-start | bytes 2097152 | tf_op jit(solution)/shard_map/psum | solution.py:11
  124.8 102.2 %all-reduce.22.cloned.1.call-start = ((), (), s32[]{:S(2)}) async-start(), calls=%async_computation.3 | async-start | bytes 1048576 | tf_op jit(solution)/shard_map/psum | solution.py:31
  181.2 138.5 %copy-start.5 = (f32[2,512,256]{1,2,0:T(8,128)S(1)}, f32[2,512,256]{1,2,0:T(8,128)}, u32[]{:S(2)}) copy-start(f32[2,512,256]{1,2,0:T(8,128)} %all-reduce.20.cloned.1.call-done) | copy-start | bytes 3145732
  182.1 86.0 %all-reduce.24.cloned.1.call-start = ((), (), s32[]{:S(2)}) async-start(), calls=%async_computation.4 | async-start | bytes 1048576 | tf_op jit(solution)/shard_map/psum | solution.py:11
  229.1 88.6 %all-reduce.26.cloned.1.call-start = ((), (), s32[]{:S(2)}) async-start(), calls=%async_computation.5 | async-start | bytes 1048576 | tf_op jit(solution)/shard_map/psum | solution.py:31
  272.1 86.7 %all-reduce.28.cloned.1.call-start = ((), (), s32[]{:S(2)}) async-start(), calls=%async_computation.6 | async-start | bytes 1048576 | tf_op jit(solution)/shard_map/psum | solution.py:11
  319.5 97.6 %all-reduce.30.cloned.1.call-start = ((), (), s32[]{:S(2)}) async-start(), calls=%async_computation.7 | async-start | bytes 1048576 | tf_op jit(solution)/shard_map/psum | solution.py:86
  362.1 95.7 %all-reduce.32.cloned.1.call-start = ((), (), s32[]{:S(2)}) async-start(), calls=%async_computation.8 | async-start | bytes 1048576 | tf_op jit(solution)/shard_map/psum | solution.py:11
  419.2 87.8 %all-reduce.34.cloned.1.call-start = ((), (), s32[]{:S(2)}) async-start(), calls=%async_computation.9 | async-start | bytes 1048576 | tf_op jit(solution)/shard_map/psum | solution.py:31
  461.5 86.9 %all-reduce.36.cloned.1.call-start = ((), (), s32[]{:S(2)}) async-start(), calls=%async_computation.10 | async-start | bytes 1048576 | tf_op jit(solution)/shard_map/psum | solution.py:62
  509.9 149.2 %all-reduce.38.cloned.1.call-start = ((), (), s32[]{:S(2)}) async-start(), calls=%async_computation.11 | async-start | bytes 3145728 | tf_op jit(solution)/shard_map/psum | solution.py:62
  548.4 16.0 %collective-permute-start = (f32[1,512,256]{1,2,0:T(8,128)}, f32[1,512,256]{1,2,0:T(8,128)S(1)}, u32[]{:S(2)}, u32[]{:S(2)}) collective-permute-start(f32[1,512,256]{1,2,0:T(8,128)} %all-reduce.36.cloned.1.call-done), channel_id=1, source_target_pairs={{0,1},{1,2},{2,3},{3,0},{4,5},{5,6},{6,7},{7,4},{8,9},{9,10},{10,1... | collective-permute-start | bytes 1572872 | tf_op jit(solution)/shard_map/ppermute | solution.py:48
  549.9 25.8 %collective-permute-start.1 = (f32[1,512,256]{1,2,0:T(8,128)}, f32[1,512,256]{1,2,0:T(8,128)S(1)}, u32[]{:S(2)}, u32[]{:S(2)}) collective-permute-start(f32[1,512,256]{1,2,0:T(8,128)} %all-reduce.36.cloned.1.call-done), channel_id=1, source_target_pairs={{0,3},{1,0},{2,1},{3,2},{4,7},{5,4},{6,5},{7,6},{8,11},{9,8},{10,9... | collective-permute-start | bytes 1572872 | tf_op jit(solution)/shard_map/ppermute | solution.py:51
  564.4 20.3 %collective-permute-start.2 = (f32[1,512,256]{1,2,0:T(8,128)S(1)}, f32[1,512,256]{1,2,0:T(8,128)S(1)}, u32[]{:S(2)}, u32[]{:S(2)}) collective-permute-start(f32[1,512,256]{1,2,0:T(8,128)S(1)} %collective-permute-done), channel_id=1, source_target_pairs={{0,1},{1,2},{2,3},{3,0},{4,5},{5,6},{6,7},{7,4},{8,9},{9,10},{10,1... | collective-permute-start | bytes 1572872 | tf_op jit(solution)/shard_map/ppermute | solution.py:48
  585.0 6.2 copy-start.6
  591.2 216.8 %all-reduce.40.cloned.1.call-start = ((), (), s32[]{:S(2)}) async-start(), calls=%async_computation.12 | async-start | bytes 1048576 | tf_op jit(solution)/shard_map/psum | solution.py:62
  659.2 39.9 %copy-start.8 = (f32[3,512,256]{1,2,0:T(8,128)S(1)}, f32[3,512,256]{1,2,0:T(8,128)}, u32[]{:S(2)}) copy-start(f32[3,512,256]{1,2,0:T(8,128)} %all-reduce.38.cloned.1.call-done) | copy-start | bytes 4718596
  659.2 38.5 %collective-permute-start.3 = (f32[3,512,256]{1,2,0:T(8,128)}, f32[3,512,256]{1,2,0:T(8,128)}, u32[]{:S(2)}, u32[]{:S(2)}) collective-permute-start(f32[3,512,256]{1,2,0:T(8,128)} %all-reduce.38.cloned.1.call-done), channel_id=1, source_target_pairs={{0,1},{1,2},{2,3},{3,0},{4,5},{5,6},{6,7},{7,4},{8,9},{9,10},{10,1... | collective-permute-start | bytes 4718600 | tf_op jit(solution)/shard_map/ppermute | solution.py:48
  660.6 70.8 %collective-permute-start.4 = (f32[3,512,256]{1,2,0:T(8,128)}, f32[3,512,256]{1,2,0:T(8,128)}, u32[]{:S(2)}, u32[]{:S(2)}) collective-permute-start(f32[3,512,256]{1,2,0:T(8,128)} %all-reduce.38.cloned.1.call-done), channel_id=1, source_target_pairs={{0,3},{1,0},{2,1},{3,2},{4,7},{5,4},{6,5},{7,6},{8,11},{9,8},{10,9... | collective-permute-start | bytes 4718600 | tf_op jit(solution)/shard_map/ppermute | solution.py:51
  697.7 65.1 %collective-permute-start.5 = (f32[3,512,256]{1,2,0:T(8,128)}, f32[3,512,256]{1,2,0:T(8,128)}, u32[]{:S(2)}, u32[]{:S(2)}) collective-permute-start(f32[3,512,256]{1,2,0:T(8,128)} %collective-permute-done.3), channel_id=1, source_target_pairs={{0,1},{1,2},{2,3},{3,0},{4,5},{5,6},{6,7},{7,4},{8,9},{9,10},{10,1... | collective-permute-start | bytes 4718600 | tf_op jit(solution)/shard_map/ppermute | solution.py:48
  699.2 67.8 %copy-start.7 = (f32[1,512,256]{1,2,0:T(8,128)S(1)}, f32[1,512,256]{1,2,0:T(8,128)}, u32[]{:S(2)}) copy-start(f32[1,512,256]{1,2,0:T(8,128)} %all-reduce.26.cloned.1.call-done) | copy-start | bytes 1572868
  764.3 2.6 copy-start.3
  770.1 129.7 %all-reduce.42.cloned.1.call-start = ((), (), s32[]{:S(2)}) async-start(), calls=%async_computation.13 | async-start | bytes 2097152 | tf_op jit(solution)/shard_map/psum | solution.py:62
  808.0 16.0 %collective-permute-start.6 = (f32[1,512,256]{1,2,0:T(8,128)}, f32[1,512,256]{1,2,0:T(8,128)S(1)}, u32[]{:S(2)}, u32[]{:S(2)}) collective-permute-start(f32[1,512,256]{1,2,0:T(8,128)} %all-reduce.40.cloned.1.call-done), channel_id=1, source_target_pairs={{0,1},{1,2},{2,3},{3,0},{4,5},{5,6},{6,7},{7,4},{8,9},{9,10},{10,1... | collective-permute-start | bytes 1572872 | tf_op jit(solution)/shard_map/ppermute | solution.py:48
  809.4 25.8 %collective-permute-start.7 = (f32[1,512,256]{1,2,0:T(8,128)}, f32[1,512,256]{1,2,0:T(8,128)S(1)}, u32[]{:S(2)}, u32[]{:S(2)}) collective-permute-start(f32[1,512,256]{1,2,0:T(8,128)} %all-reduce.40.cloned.1.call-done), channel_id=1, source_target_pairs={{0,3},{1,0},{2,1},{3,2},{4,7},{5,4},{6,5},{7,6},{8,11},{9,8},{10,9... | collective-permute-start | bytes 1572872 | tf_op jit(solution)/shard_map/ppermute | solution.py:51
  823.9 20.3 %collective-permute-start.8 = (f32[1,512,256]{1,2,0:T(8,128)S(1)}, f32[1,512,256]{1,2,0:T(8,128)S(1)}, u32[]{:S(2)}, u32[]{:S(2)}) collective-permute-start(f32[1,512,256]{1,2,0:T(8,128)S(1)} %collective-permute-done.6), channel_id=1, source_target_pairs={{0,1},{1,2},{2,3},{3,0},{4,5},{5,6},{6,7},{7,4},{8,9},{9,10},{10,1... | collective-permute-start | bytes 1572872 | tf_op jit(solution)/shard_map/ppermute | solution.py:48
  849.2 176.6 %all-reduce.44.cloned.1.call-start = ((), (), s32[]{:S(2)}) async-start(), calls=%async_computation.14 | async-start | bytes 2097152 | tf_op jit(solution)/shard_map/psum | solution.py:62
  899.8 28.2 %copy-start.10 = (f32[2,512,256]{1,2,0:T(8,128)S(1)}, f32[2,512,256]{1,2,0:T(8,128)}, u32[]{:S(2)}) copy-start(f32[2,512,256]{1,2,0:T(8,128)} %all-reduce.42.cloned.1.call-done) | copy-start | bytes 3145732
  899.8 27.1 %collective-permute-start.9 = (f32[2,512,256]{1,2,0:T(8,128)}, f32[2,512,256]{1,2,0:T(8,128)S(1)}, u32[]{:S(2)}, u32[]{:S(2)}) collective-permute-start(f32[2,512,256]{1,2,0:T(8,128)} %all-reduce.42.cloned.1.call-done), channel_id=1, source_target_pairs={{0,1},{1,2},{2,3},{3,0},{4,5},{5,6},{6,7},{7,4},{8,9},{9,10},{10,1... | collective-permute-start | bytes 3145736 | tf_op jit(solution)/shard_map/ppermute | solution.py:48
  901.3 48.1 %collective-permute-start.10 = (f32[2,512,256]{1,2,0:T(8,128)}, f32[2,512,256]{1,2,0:T(8,128)S(1)}, u32[]{:S(2)}, u32[]{:S(2)}) collective-permute-start(f32[2,512,256]{1,2,0:T(8,128)} %all-reduce.42.cloned.1.call-done), channel_id=1, source_target_pairs={{0,3},{1,0},{2,1},{3,2},{4,7},{5,4},{6,5},{7,6},{8,11},{9,8},{10,9... | collective-permute-start | bytes 3145736 | tf_op jit(solution)/shard_map/ppermute | solution.py:51
  927.0 44.0 %collective-permute-start.11 = (f32[2,512,256]{1,2,0:T(8,128)S(1)}, f32[2,512,256]{1,2,0:T(8,128)S(1)}, u32[]{:S(2)}, u32[]{:S(2)}) collective-permute-start(f32[2,512,256]{1,2,0:T(8,128)S(1)} %collective-permute-done.9), channel_id=1, source_target_pairs={{0,1},{1,2},{2,3},{3,0},{4,5},{5,6},{6,7},{7,4},{8,9},{9,10},{10,1... | collective-permute-start | bytes 3145736 | tf_op jit(solution)/shard_map/ppermute | solution.py:48
  928.1 43.1 %copy-start.2 = (f32[1,3,512,512]{3,2,1,0:T(8,128)S(1)}, f32[1,3,512,512]{3,2,1,0:T(8,128)}, u32[]{:S(2)}) copy-start(f32[1,3,512,512]{3,2,1,0:T(8,128)} %param.6) | copy-start | bytes 9437188
  928.1 43.1 %copy-start.4 = (f32[2,512,256]{1,2,0:T(8,128)S(1)}, f32[2,512,256]{1,2,0:T(8,128)}, u32[]{:S(2)}) copy-start(f32[2,512,256]{1,2,0:T(8,128)} %all-reduce.18.cloned.1.call-done) | copy-start | bytes 3145732
  1025.8 28.2 %copy-start.9 = (f32[2,512,256]{1,2,0:T(8,128)S(1)}, f32[2,512,256]{1,2,0:T(8,128)}, u32[]{:S(2)}) copy-start(f32[2,512,256]{1,2,0:T(8,128)} %all-reduce.44.cloned.1.call-done) | copy-start | bytes 3145732
  1025.8 27.1 %collective-permute-start.12 = (f32[2,512,256]{1,2,0:T(8,128)}, f32[2,512,256]{1,2,0:T(8,128)S(1)}, u32[]{:S(2)}, u32[]{:S(2)}) collective-permute-start(f32[2,512,256]{1,2,0:T(8,128)} %all-reduce.44.cloned.1.call-done), channel_id=1, source_target_pairs={{0,1},{1,2},{2,3},{3,0},{4,5},{5,6},{6,7},{7,4},{8,9},{9,10},{10,1... | collective-permute-start | bytes 3145736 | tf_op jit(solution)/shard_map/ppermute | solution.py:48
  1027.2 48.1 %collective-permute-start.13 = (f32[2,512,256]{1,2,0:T(8,128)}, f32[2,512,256]{1,2,0:T(8,128)S(1)}, u32[]{:S(2)}, u32[]{:S(2)}) collective-permute-start(f32[2,512,256]{1,2,0:T(8,128)} %all-reduce.44.cloned.1.call-done), channel_id=1, source_target_pairs={{0,3},{1,0},{2,1},{3,2},{4,7},{5,4},{6,5},{7,6},{8,11},{9,8},{10,9... | collective-permute-start | bytes 3145736 | tf_op jit(solution)/shard_map/ppermute | solution.py:51
  1052.9 44.0 %collective-permute-start.14 = (f32[2,512,256]{1,2,0:T(8,128)S(1)}, f32[2,512,256]{1,2,0:T(8,128)S(1)}, u32[]{:S(2)}, u32[]{:S(2)}) collective-permute-start(f32[2,512,256]{1,2,0:T(8,128)S(1)} %collective-permute-done.12), channel_id=1, source_target_pairs={{0,1},{1,2},{2,3},{3,0},{4,5},{5,6},{6,7},{7,4},{8,9},{9,10},{10,1... | collective-permute-start | bytes 3145736 | tf_op jit(solution)/shard_map/ppermute | solution.py:48
  1096.9 2.0 copy-start.1
Sparse Core Ops, SparseCore 0:
  11.0 54.5 all-reduce.15
  70.5 51.9 all-reduce.17
  125.5 51.8 all-reduce.19
  182.2 44.6 all-reduce.21
  229.7 38.2 all-reduce.23
  272.3 45.3 all-reduce.25
  320.6 38.2 all-reduce.27
  362.6 54.5 all-reduce.29
  420.2 37.5 all-reduce.31
  461.7 45.3 all-reduce.33
  510.1 38.2 all-reduce.35
  591.3 67.8 all-reduce.37
  770.2 37.6 all-reduce.39
  849.3 50.5 all-reduce.41
  975.5 50.2 all-reduce.43
